TPU v7x, 32 devices: a whole 2x2x4 slice. The times are simulated.
32 devices in a mesh: dp: 16 (over z, x, core), tensor: 2 (over y).
Axes of the slice: x: 2, y: 2, z: 4, core: 2. Of those that a mesh axis runs over, the one named last changes fastest.
Arguments:
- tokens: bfloat16 [1024, 16, 1152], P('tensor', 'dp'), may hold values from -6 to 6
- cond: bfloat16 [16, 1152], P('dp'), may hold values from -6 to 6
- mod_weight: bfloat16 [1152, 6912], P('dp'), may hold values from -0.1875 to 0.1875
- mod_bias: bfloat16 [6912], replicated, may hold values from -3 to 3
- query_key_value_weight: bfloat16 [1152, 3, 1152], P('dp', None, 'tensor'), may hold values from -0.1875 to 0.1875
- qkv_bias: bfloat16 [2, 1152], P(None, 'tensor'), may hold values from -3 to 3
- attention_out_weight: bfloat16 [1152, 1152], P('tensor', 'dp'), may hold values from -1.5 to 1.5
- attention_out_bias: bfloat16 [1152], replicated, may hold values from -3 to 3
- first_hidden_weight: bfloat16 [1152, 4608], P('dp', 'tensor'), may hold values from -0.1875 to 0.1875
- first_hidden_bias: bfloat16 [4608], P('tensor'), may hold values from -3 to 3
- second_hidden_weight: bfloat16 [4608, 1152], P('tensor', 'dp'), may hold values from -0.09375 to 0.09375
- second_hidden_bias: bfloat16 [1152], replicated, may hold values from -3 to 3
- out_grad: bfloat16 [1024, 16, 1152], P('tensor', 'dp'), may hold values from -6 to 6
Outputs:
- output: bfloat16 [1024, 16, 1152], P('tensor', 'dp')
- tokens_grad: bfloat16 [1024, 16, 1152], P('tensor', 'dp')
- cond_grad: float32 [16, 1152], P('dp')
- mod_weight_grad: float32 [1152, 6912], P('dp')
- mod_bias_grad: float32 [6912], replicated
- qkv_weight_grad: float32 [1152, 3, 1152], P('dp', None, 'tensor')
- qkv_bias_grad: float32 [2, 1152], P(None, 'tensor')
- proj_weight_grad: float32 [1152, 1152], P('tensor', 'dp')
- proj_bias_grad: float32 [1152], replicated
- fc1_weight_grad: float32 [1152, 4608], P('dp', 'tensor')
- fc1_bias_grad: float32 [4608], P('tensor')
- fc2_weight_grad: float32 [4608, 1152], P('tensor', 'dp')
- fc2_bias_grad: float32 [1152], replicated
All inputs are finite; a program needn't handle non-finite values.
Results may differ from a plain program's by a relative error of at most 0.02.
The roundings to bfloat16 on the way count: a program that leaves them out, or rounds other values in their place, can miss the bound.
Values may be sent and summed in bfloat16 or wider, within the bound.
A program may use at most 256 MiB of HBM per device.

v0:
```python
import jax
import jax.numpy as jnp
from jax import lax
from jax.sharding import PartitionSpec as P

HEADS = 16


def modulate(hidden, shifts, scales):
    center = hidden - jnp.mean(hidden, axis=-1, keepdims=True)
    spread = jnp.mean(center * center, axis=-1, keepdims=True)
    return center * lax.rsqrt(spread + 1e-06) * (1.0 + scales) + shifts


def gelu_tanh(values):
    return jax.nn.gelu(values, approximate=True)


def attend_forward(packed):
    queries = packed[:, 0]
    keys_all = packed[:, 1]
    values_all = packed[:, 2]
    seq_len = packed.shape[0]
    scaling = packed.shape[3] ** (-0.5)
    block_rows = min(512, seq_len)
    results = []
    log_parts = []
    for offset in range(0, seq_len, block_rows):
        query_block = queries[offset : offset + block_rows]
        scores = (
            jnp.einsum("qhe,khe->hqk", query_block, keys_all, preferred_element_type=jnp.float32)
            * scaling
        )
        highest = jnp.max(scores, axis=-1, keepdims=True)
        weights = jnp.exp(scores - highest)
        row_total = jnp.sum(weights, axis=-1, keepdims=True)
        prob_low = (weights / row_total).astype(jnp.bfloat16)
        mixture = jnp.einsum(
            "hqk,khe->qhe", prob_low, values_all, preferred_element_type=jnp.float32
        )
        results.append(mixture.reshape(block_rows, -1))
        log_parts.append((highest + jnp.log(row_total))[..., 0])
    return (jnp.concatenate(results, 0).astype(jnp.bfloat16), jnp.concatenate(log_parts, 1))


def attend_backward(inputs):
    packed, grad_out, log_totals = inputs
    queries = packed[:, 0]
    keys_all = packed[:, 1]
    values_all = packed[:, 2]
    seq_len = packed.shape[0]
    scaling = packed.shape[3] ** (-0.5)
    block_rows = min(512, seq_len)
    query_grads = []
    key_grad = jnp.zeros(keys_all.shape, jnp.float32)
    value_grad = jnp.zeros(values_all.shape, jnp.float32)
    for offset in range(0, seq_len, block_rows):
        query_block = queries[offset : offset + block_rows]
        grad_block = grad_out[offset : offset + block_rows]
        scores = (
            jnp.einsum("qhe,khe->hqk", query_block, keys_all, preferred_element_type=jnp.float32)
            * scaling
        )
        probs = jnp.exp(scores - log_totals[:, offset : offset + block_rows, None])
        prob_low = probs.astype(jnp.bfloat16)
        prob_grad = jnp.einsum(
            "qhe,khe->hqk", grad_block, values_all, preferred_element_type=jnp.float32
        )
        inner = jnp.sum(probs * prob_grad, axis=-1, keepdims=True)
        score_grad = (probs * (prob_grad - inner)).astype(jnp.bfloat16)
        query_grads.append(
            jnp.einsum("hqk,khe->qhe", score_grad, keys_all, preferred_element_type=jnp.float32)
            * scaling
        )
        key_grad = (
            key_grad
            + jnp.einsum(
                "hqk,qhe->khe", score_grad, query_block, preferred_element_type=jnp.float32
            )
            * scaling
        )
        value_grad = value_grad + jnp.einsum(
            "hqk,qhe->khe", prob_low, grad_block, preferred_element_type=jnp.float32
        )
    return jnp.stack([jnp.concatenate(query_grads, 0), key_grad, value_grad], 1).astype(
        jnp.bfloat16
    )


def on_device(
    tokens,
    cond,
    mod_weight,
    mod_bias,
    query_key_value_weight,
    qkv_bias,
    attention_out_weight,
    attention_out_bias,
    first_hidden_weight,
    first_hidden_bias,
    second_hidden_weight,
    second_hidden_bias,
    out_grad,
):
    w_mod, w_qkv, w_proj, w_fc1, w_fc2 = (
        lax.all_gather(mod_weight, "dp", axis=0, tiled=True),
        lax.all_gather(query_key_value_weight, "dp", axis=0, tiled=True),
        lax.all_gather(attention_out_weight, "dp", axis=1, tiled=True),
        lax.all_gather(first_hidden_weight, "dp", axis=0, tiled=True),
        lax.all_gather(second_hidden_weight, "dp", axis=1, tiled=True),
    )
    seq_local, latents, width = tokens.shape
    columns = query_key_value_weight.shape[2]
    head_size = width // HEADS
    heads_here = columns // head_size
    local_rows = seq_local * latents
    cond_wide = cond.astype(jnp.float32)
    silu_cond, silu_back = jax.vjp(jax.nn.silu, cond_wide)
    silu_low = silu_cond.astype(jnp.bfloat16)
    modulation = jnp.dot(silu_low, w_mod, preferred_element_type=jnp.float32) + mod_bias.astype(
        jnp.float32
    )
    pieces = modulation.reshape(latents, 6, width)
    hidden_in = tokens.astype(jnp.float32)
    attention_normalized, norm_a_back = jax.vjp(modulate, hidden_in, pieces[:, 0], pieces[:, 1])
    gathered_a = lax.all_gather(
        attention_normalized.astype(jnp.bfloat16), "tensor", axis=0, tiled=True
    )
    seq_len = gathered_a.shape[0]
    total_rows = seq_len * latents
    rows_a = gathered_a.reshape(total_rows, width)
    qkv_flat = w_qkv.reshape(width, 3 * columns)
    zero_row = jnp.zeros((columns,), jnp.float32)
    query_key_value_shift = jnp.stack(
        [qkv_bias[0].astype(jnp.float32), zero_row, qkv_bias[1].astype(jnp.float32)]
    )
    projected_output = (
        jnp.dot(rows_a, qkv_flat, preferred_element_type=jnp.float32).reshape(
            seq_len, latents, 3, columns
        )
        + query_key_value_shift
    )
    packed = jnp.moveaxis(projected_output.astype(jnp.bfloat16), 1, 0).reshape(
        latents, seq_len, 3, heads_here, head_size
    )
    attention_result, log_totals = lax.map(attend_forward, packed)
    attended_rows = jnp.moveaxis(attention_result, 0, 1).reshape(total_rows, columns)
    summed_a = lax.psum_scatter(
        jnp.dot(attended_rows, w_proj, preferred_element_type=jnp.float32).astype(jnp.bfloat16),
        "tensor",
        scatter_dimension=0,
        tiled=True,
    ).astype(jnp.float32)
    attention_branch = summed_a.reshape(seq_local, latents, width) + attention_out_bias.astype(
        jnp.float32
    )
    resid_mid = hidden_in + pieces[:, 2] * attention_branch
    feedforward_normalized, norm_m_back = jax.vjp(modulate, resid_mid, pieces[:, 3], pieces[:, 4])
    gathered_m = lax.all_gather(
        feedforward_normalized.astype(jnp.bfloat16), "tensor", axis=0, tiled=True
    )
    rows_m = gathered_m.reshape(total_rows, width)
    before_activation = jnp.dot(
        rows_m, w_fc1, preferred_element_type=jnp.float32
    ) + first_hidden_bias.astype(jnp.float32)
    gelu_activated, gelu_back = jax.vjp(gelu_tanh, before_activation)
    act_low = gelu_activated.astype(jnp.bfloat16)
    summed_m = lax.psum_scatter(
        jnp.dot(act_low, w_fc2, preferred_element_type=jnp.float32).astype(jnp.bfloat16),
        "tensor",
        scatter_dimension=0,
        tiled=True,
    ).astype(jnp.float32)
    feedforward_branch = summed_m.reshape(seq_local, latents, width) + second_hidden_bias.astype(
        jnp.float32
    )
    output = (resid_mid + pieces[:, 5] * feedforward_branch).astype(jnp.bfloat16)
    grad_out = out_grad.astype(jnp.float32)
    gate_m_grad = jnp.sum(grad_out * feedforward_branch, axis=0)
    grad_m_low = (grad_out * pieces[:, 5]).astype(jnp.bfloat16)
    grad_m_rows = lax.all_gather(grad_m_low, "tensor", axis=0, tiled=True).reshape(
        total_rows, width
    )
    fc2_bias_grad = jnp.sum(grad_m_rows, axis=0, dtype=jnp.float32)
    fc2_weight_grad = jnp.einsum(
        "rf,rd->fd", act_low, grad_m_rows, preferred_element_type=jnp.float32
    )
    act_grad = jnp.einsum("rd,fd->rf", grad_m_rows, w_fc2, preferred_element_type=jnp.float32)
    pre_grad = gelu_back(act_grad)[0].astype(jnp.bfloat16)
    fc1_bias_grad = jnp.sum(pre_grad, axis=0, dtype=jnp.float32)
    fc1_weight_grad = jnp.einsum("rd,rf->df", rows_m, pre_grad, preferred_element_type=jnp.float32)
    normed_m_grad = (
        lax.psum_scatter(
            jnp.einsum("rf,df->rd", pre_grad, w_fc1, preferred_element_type=jnp.float32).astype(
                jnp.bfloat16
            ),
            "tensor",
            scatter_dimension=0,
            tiled=True,
        )
        .astype(jnp.float32)
        .reshape(seq_local, latents, width)
    )
    resid_part, shift_m_grad, scale_m_grad = norm_m_back(normed_m_grad)
    resid_grad = grad_out + resid_part
    gate_a_grad = jnp.sum(resid_grad * attention_branch, axis=0)
    grad_a_low = (resid_grad * pieces[:, 2]).astype(jnp.bfloat16)
    grad_a_flat = grad_a_low.reshape(local_rows, width)
    proj_bias_part = jnp.sum(grad_a_flat, axis=0, dtype=jnp.float32)
    grad_a_rows = lax.all_gather(grad_a_low, "tensor", axis=0, tiled=True).reshape(
        total_rows, width
    )
    proj_weight_grad = jnp.einsum(
        "rc,rd->cd", attended_rows, grad_a_rows, preferred_element_type=jnp.float32
    )
    attended_grad = jnp.einsum(
        "rd,cd->rc", grad_a_rows, w_proj, preferred_element_type=jnp.float32
    ).astype(jnp.bfloat16)
    grad_packed = jnp.moveaxis(attended_grad.reshape(seq_len, latents, heads_here, head_size), 1, 0)
    qkv_grad_packed = lax.map(attend_backward, (packed, grad_packed, log_totals))
    qkv_grad_rows = jnp.moveaxis(qkv_grad_packed, 0, 1).reshape(total_rows, 3 * columns)
    bias_sums = jnp.sum(qkv_grad_rows.reshape(total_rows, 3, columns), axis=0, dtype=jnp.float32)
    qkv_bias_grad = jnp.stack([bias_sums[0], bias_sums[2]])
    qkv_weight_grad = jnp.einsum(
        "rd,rc->dc", rows_a, qkv_grad_rows, preferred_element_type=jnp.float32
    ).reshape(width, 3, columns)
    normed_a_grad = (
        lax.psum_scatter(
            jnp.einsum(
                "rc,dc->rd", qkv_grad_rows, qkv_flat, preferred_element_type=jnp.float32
            ).astype(jnp.bfloat16),
            "tensor",
            scatter_dimension=0,
            tiled=True,
        )
        .astype(jnp.float32)
        .reshape(seq_local, latents, width)
    )
    input_part, shift_a_grad, scale_a_grad = norm_a_back(normed_a_grad)
    tokens_grad = (resid_grad + input_part).astype(jnp.bfloat16)
    partial_mod = jnp.stack(
        [shift_a_grad, scale_a_grad, gate_a_grad, shift_m_grad, scale_m_grad, gate_m_grad], 1
    ).reshape(latents, 6 * width)
    mod_summed, proj_bias_grad = (
        lax.psum(partial_mod.astype(jnp.bfloat16), "tensor").astype(jnp.float32),
        lax.psum(proj_bias_part.astype(jnp.bfloat16), "tensor").astype(jnp.float32),
    )
    mod_grad_low = mod_summed.astype(jnp.bfloat16)
    silu_grad = jnp.einsum("le,de->ld", mod_grad_low, w_mod, preferred_element_type=jnp.float32)
    cond_grad = silu_back(silu_grad)[0]
    silu_every, mod_every = (
        lax.all_gather(silu_low, "dp", axis=0, tiled=True),
        lax.all_gather(mod_grad_low, "dp", axis=0, tiled=True),
    )
    owned_rows = mod_weight.shape[0]
    silu_owned = lax.dynamic_slice_in_dim(
        silu_every, lax.axis_index("dp") * owned_rows, owned_rows, 1
    )
    mod_weight_grad = jnp.einsum(
        "ld,le->de", silu_owned, mod_every, preferred_element_type=jnp.float32
    )
    mod_bias_grad = jnp.sum(mod_every, axis=0, dtype=jnp.float32)
    qkv_weight_grad, proj_weight_grad, fc1_weight_grad, fc2_weight_grad = (
        lax.psum_scatter(
            qkv_weight_grad.astype(jnp.bfloat16), "dp", scatter_dimension=0, tiled=True
        ).astype(jnp.float32),
        lax.psum_scatter(
            proj_weight_grad.astype(jnp.bfloat16), "dp", scatter_dimension=1, tiled=True
        ).astype(jnp.float32),
        lax.psum_scatter(
            fc1_weight_grad.astype(jnp.bfloat16), "dp", scatter_dimension=0, tiled=True
        ).astype(jnp.float32),
        lax.psum_scatter(
            fc2_weight_grad.astype(jnp.bfloat16), "dp", scatter_dimension=1, tiled=True
        ).astype(jnp.float32),
    )
    qkv_bias_grad, proj_bias_grad, fc1_bias_grad, fc2_bias_grad = lax.psum(
        (qkv_bias_grad, proj_bias_grad, fc1_bias_grad, fc2_bias_grad), "dp"
    )
    return (
        output,
        tokens_grad,
        cond_grad,
        mod_weight_grad,
        mod_bias_grad,
        qkv_weight_grad,
        qkv_bias_grad,
        proj_weight_grad,
        proj_bias_grad,
        fc1_weight_grad,
        fc1_bias_grad,
        fc2_weight_grad,
        fc2_bias_grad,
    )


def solution(mesh):
    return jax.shard_map(
        on_device,
        mesh=mesh,
        in_specs=(
            P("tensor", "dp", None),
            P("dp", None),
            P("dp", None),
            P(),
            P("dp", None, "tensor"),
            P(None, "tensor"),
            P("tensor", "dp"),
            P(),
            P("dp", "tensor"),
            P("tensor"),
            P("tensor", "dp"),
            P(),
            P("tensor", "dp", None),
        ),
        out_specs=(
            P("tensor", "dp", None),
            P("tensor", "dp", None),
            P("dp", None),
            P("dp", None),
            P(),
            P("dp", None, "tensor"),
            P(None, "tensor"),
            P("tensor", "dp"),
            P(),
            P("dp", "tensor"),
            P("tensor"),
            P("tensor", "dp"),
            P(),
        ),
        check_vma=False,
    )
```

profile of v0, /device:TPU:0, one launch (start us, length us, event | category | flops | bytes accessed | tf_op | source)
XLA Modules:
  0.0 1025.1 jit_solution(3620825164057800775)
XLA Ops:
  10.7 123.7 %all-gather.12.cloned.1.call-done = bf16[1152,6912]{1,0:T(8,128)(2,1)} async-done(((bf16[72,6912]{1,0:T(8,128)(2,1)}), bf16[1152,6912]{1,0:T(8,128)(2,1)}) %all-gather.12.cloned.1.call-update) | async-done | bytes 15925264 | tf_op jit(solution)/shard_map/all_gather | solution.py:106
  134.5 7.7 convolution_reduce_fusion
  145.8 40.8 %all-gather.16.cloned.1.call-done = bf16[1152,3,576]{2,0,1:T(8,128)(2,1)} async-done(((bf16[72,3,576]{2,0,1:T(8,128)(2,1)}), bf16[1152,3,576]{2,0,1:T(8,128)(2,1)}) %all-gather.16.cloned.1.call-update) | async-done | bytes 3981328 | tf_op jit(solution)/shard_map/all_gather | solution.py:107
  186.6 6.5 copy.29
  193.1 30.2 %all-gather.14.cloned.1.call-done = bf16[1024,1,1152]{2,0,1:T(8,128)(2,1)} async-done(((bf16[512,1,1152]{2,0,1:T(8,128)(2,1)}), bf16[1024,1,1152]{2,0,1:T(8,128)(2,1)}) %all-gather.14.cloned.1.call-update) | async-done | bytes 2359312 | tf_op jit(solution)/shard_map/all_gather | solution.py:126
  223.3 7.6 add_convert_fusion
  231.0 8.1 multiply_reduce_fusion.2
  241.7 13.6 %fusion.1 = f32[8,512]{1,0:T(8,128)S(1)} fusion(f32[8,512,1024]{2,1,0:T(8,128)} %get-tuple-element.73, f32[8,512]{1,0:T(8,128)S(1)} %get-tuple-element.72), kind=kLoop, calls=%fused_computation.11 | loop fusion | flops 12578816 | bytes 16809984 | tf_op jit(solution)/shard_map/while/body/eval_jaxpr/reduce_sum | solution.py:36
  255.3 7.9 fusion.75
  263.2 3.9 fusion
  267.6 4.7 fusion.76
  272.4 5.2 convolution_convert_fusion.6
  278.3 34.3 %reduce-scatter.13.cloned.1.call-done = bf16[512,1152]{1,0:T(8,128)(2,1)} async-done(((bf16[1024,1152]{1,0:T(8,128)(2,1)}), bf16[512,1152]{1,0:T(8,128)(2,1)}) %reduce-scatter.13.cloned.1.call-update) | async-done | bytes 1179664 | tf_op jit(solution)/shard_map/reduce_scatter | solution.py:148
  321.7 49.5 %all-gather.22.cloned.1.call-done = bf16[1152,2304]{1,0:T(8,128)(2,1)} async-done(((bf16[72,2304]{1,0:T(8,128)(2,1)}), bf16[1152,2304]{1,0:T(8,128)(2,1)}) %all-gather.22.cloned.1.call-update) | async-done | bytes 5308432 | tf_op jit(solution)/shard_map/all_gather | solution.py:109
  371.2 36.9 %all-gather.20.cloned.1.call-done = bf16[1024,1,1152]{2,0,1:T(8,128)(2,1)} async-done(((bf16[512,1,1152]{2,0,1:T(8,128)(2,1)}), bf16[1024,1,1152]{2,0,1:T(8,128)(2,1)}) %all-gather.20.cloned.1.call-update) | async-done | bytes 2359312 | tf_op jit(solution)/shard_map/all_gather | solution.py:159
  408.1 11.7 %fusion.57 = f32[1024,2304]{1,0:T(8,128)} fusion(bf16[1152,2304]{1,0:T(8,128)(2,1)} %all-gather.22.cloned.1.call-done, bf16[1024,1,1152]{2,0,1:T(8,128)(2,1)} %all-gather.20.cloned.1.call-done), kind=kOutput, calls=%fused_computation.98 | convolution fusion | flops 5435817984 | bytes 17104896 | tf_op jit(solution)/shard_map/dot_general | solution.py:163
  419.7 47.1 %all-gather.24.cloned.1.call-done = bf16[2304,1152]{0,1:T(8,128)(2,1)} async-done(((bf16[2304,72]{0,1:T(8,128)(2,1)}), bf16[2304,1152]{0,1:T(8,128)(2,1)}) %all-gather.24.cloned.1.call-update) | async-done | bytes 5308432 | tf_op jit(solution)/shard_map/all_gather | solution.py:110
  466.9 36.9 %all-gather.26.cloned.1.call-done = bf16[1024,1,1152]{2,0,1:T(8,128)(2,1)} async-done(((bf16[512,1,1152]{2,0,1:T(8,128)(2,1)}), bf16[1024,1,1152]{2,0,1:T(8,128)(2,1)}) %all-gather.26.cloned.1.call-update) | async-done | bytes 2359312 | tf_op jit(solution)/shard_map/all_gather | solution.py:181
  503.7 15.4 %convert_reduce_fusion = (f32[2304]{0:T(1024)}, bf16[1024,2304]{1,0:T(8,128)(2,1)S(1)}) fusion(f32[1024,2304]{1,0:T(8,128)} %fusion.57, f32[2304]{0:T(1024)} %convert_element_type.198, bf16[2304,1152]{0,1:T(8,128)(2,1)} %all-gather.24.cloned.1.call-done, bf16[1024,1,1152]{2,0,1:T(8,128)(2,1)} %all-gather.26.cloned.1.call-done), kind=kOutput, calls=%fused_computation.27 | convolution fusion | flops 5490079744 | bytes 21841920 | tf_op jit(solution)/shard_map/rd,fd->rf/dot_general | solution.py:188
  521.4 10.0 convolution_convert_fusion.3
  531.8 34.4 %reduce-scatter.17.cloned.1.call-done = bf16[512,1152]{1,0:T(8,128)(2,1)} async-done(((bf16[1024,1152]{1,0:T(8,128)(2,1)}), bf16[512,1152]{1,0:T(8,128)(2,1)}) %reduce-scatter.17.cloned.1.call-update) | async-done | bytes 1179664 | tf_op jit(solution)/shard_map/reduce_scatter | solution.py:193
  573.7 10.9 %convolution_convert_fusion = bf16[2304,1152]{0,1:T(8,128)(2,1)} fusion(bf16[1024,1,1152]{2,0,1:T(8,128)(2,1)S(1)} %copy-done.24, f32[1024,2304]{1,0:T(8,128)} %fusion.57, f32[2304]{0:T(1024)} %convert_element_type.198), kind=kOutput, calls=%fused_computation.16 | convolution fusion | flops 5462065152 | bytes 17114112 | tf_op jit(solution)/shard_map/rf,rd->fd/dot_general | solution.py:185
  586.3 9.7 convolution_convert_fusion.1
  596.0 13.1 %all-gather.28.cloned.1.call-done = bf16[1024,1,1152]{2,0,1:T(8,128)(2,1)} async-done(((bf16[512,1,1152]{2,0,1:T(8,128)(2,1)}), bf16[1024,1,1152]{2,0,1:T(8,128)(2,1)}) %all-gather.28.cloned.1.call-update) | async-done | bytes 2359312 | tf_op jit(solution)/shard_map/all_gather | solution.py:210
  613.5 15.2 %multiply_reduce_fusion.1 = (f32[8,512]{1,0:T(8,128)S(1)}, f32[8,512,1024]{2,1,0:T(8,128)}) fusion(f32[8,512,1024]{2,1,0:T(8,128)} %copy-done, f32[8,512]{1,0:T(8,128)S(1)} %log_add_fusion.1, bf16[512,8,72]{0,2,1:T(8,128)(2,1)S(1)} %bitcast.230, bf16[1024,3,8,72]{0,3,2,1:T(8,128)(2,1)} %bitcast.220), kind=kOutput, calls=%fused_computation.4 | convolution fusion | flops 620752896 | bytes 35356672 | tf_op jit(solution)/shard_map/while/body/eval_jaxpr/qhe,khe->hqk/dot_general | solution.py:66
  631.7 11.0 %multiply_convert_fusion.1 = bf16[8,512,1024]{2,1,0:T(8,128)(2,1)} fusion(f32[8,512,1024]{2,1,0:T(8,128)} %get-tuple-element.77, f32[8,512,1024]{2,1,0:T(8,128)S(1)} %bitcast.213, f32[8,512]{1,0:T(8,128)S(1)} %get-tuple-element.76, f32[8,512]{1,0:T(8,128)S(1)} %log_add_fusion.1), kind=kLoop, calls=%fused_computation.3 | loop fusion | flops 20971520 | bytes 41975808 | tf_op jit(solution)/shard_map/while/body/eval_jaxpr/convert_element_type | solution.py:70
  646.0 6.5 fusion.82
  652.5 3.5 fusion.73
  656.0 12.1 %multiply_reduce_fusion = (f32[8,512]{1,0:T(8,128)}, f32[8,512,1024]{2,1,0:T(8,128)}) fusion(f32[8,512,1024]{2,1,0:T(8,128)} %get-tuple-element.73, f32[8,512]{1,0:T(8,128)S(1)} %copy-done.29, bf16[512,8,72]{0,2,1:T(8,128)(2,1)S(1)} %bitcast.232, bf16[1024,3,8,72]{0,3,2,1:T(8,128)(2,1)S(1)} %bitcast.225), kind=kOutput, calls=%fused_computation.1 | convolution fusion | flops 620752896 | bytes 35356672 | tf_op jit(solution)/shard_map/while/body/eval_jaxpr/qhe,khe->hqk/dot_general | solution.py:66
  668.1 13.1 %multiply_convert_fusion = bf16[8,512,1024]{2,1,0:T(8,128)(2,1)S(1)} fusion(f32[8,512,1024]{2,1,0:T(8,128)} %get-tuple-element.79, f32[8,512,1024]{2,1,0:T(8,128)} %get-tuple-element.73, f32[8,512]{1,0:T(8,128)} %get-tuple-element.78, f32[8,512]{1,0:T(8,128)} %log_add_fusion), kind=kLoop, calls=%fused_computation | loop fusion | flops 20971520 | bytes 41975808 | tf_op jit(solution)/shard_map/while/body/eval_jaxpr/convert_element_type | solution.py:70
  684.7 4.0 fusion.74
  688.8 7.6 fusion.11
  696.5 4.3 fusion.67
  702.9 5.8 add_multiply_fusion
  712.4 6.3 convolution_convert_fusion.5
  719.4 13.8 %convolution_convert_fusion.4 = bf16[1024,1152]{1,0:T(8,128)(2,1)} fusion(bf16[2304,1152]{0,1:T(8,128)(2,1)} %all-gather.24.cloned.1.call-done, f32[1024,2304]{1,0:T(8,128)} %fusion.57, f32[2304]{0:T(1024)S(1)} %copy-done.59), kind=kOutput, calls=%fused_computation.45 | convolution fusion | flops 5460590592 | bytes 17114112 | tf_op jit(solution)/shard_map/dot_general | solution.py:169
  734.9 7.6 convolution_convert_fusion.2
  742.5 18.2 %copy.34 = bf16[1152,3,576]{2,1,0:T(4,128)(2,1)} copy(bf16[1152,3,576]{2,0,1:T(8,128)(2,1)S(1)} %convolution_convert_fusion.2) | data formatting | bytes 7962624
  760.7 12.3 %reshape.346 = bf16[1152,1728]{1,0:T(8,128)(2,1)} reshape(bf16[1152,3,576]{2,1,0:T(4,128)(2,1)} %copy.34) | data formatting | bytes 7962624
  774.3 21.5 %all-gather = bf16[16,1,1152]{2,1,0:T(2,128)(2,1)S(1)} all-gather(bf16[1,1,1152]{2,1,0:T(2,128)(2,1)S(1)} %convert_bitcast_fusion.2), channel_id=1, replica_groups=mesh['dp'=16,'tensor'=2] {'dp'}, dimensions={0}, use_global_device_ids=true | all-gather | bytes 39168 | tf_op jit(solution)/shard_map/all_gather | solution.py:252
  806.9 30.5 %reduce-scatter.27.cloned.1.call-done = bf16[576,72]{0,1:T(8,128)(2,1)} async-done(((bf16[576,1152]{0,1:T(8,128)(2,1)}), bf16[576,72]{0,1:T(8,128)(2,1)}) %reduce-scatter.27.cloned.1.call-update) | async-done | bytes 82960
  839.0 34.2 %reduce-scatter.19.cloned.1.call-done = bf16[512,1152]{1,0:T(8,128)(2,1)} async-done(((bf16[1024,1152]{1,0:T(8,128)(2,1)}), bf16[512,1152]{1,0:T(8,128)(2,1)}) %reduce-scatter.19.cloned.1.call-update) | async-done | bytes 1179664 | tf_op jit(solution)/shard_map/reduce_scatter | solution.py:228
  881.7 28.4 %reduce-scatter.15.cloned.1.call-done = bf16[512,1152]{1,0:T(8,128)(2,1)} async-done(((bf16[1024,1152]{1,0:T(8,128)(2,1)}), bf16[512,1152]{1,0:T(8,128)(2,1)}) %reduce-scatter.15.cloned.1.call-update) | async-done | bytes 1179664 | tf_op jit(solution)/shard_map/reduce_scatter | solution.py:168
  910.1 5.1 fusion.45
  916.1 7.8 all-reduce.2
  923.8 60.7 %all-reduce.1 = (f32[2,576]{1,0:T(2,128)}, f32[1152]{0:T(1024)}, f32[2304]{0:T(1024)}, f32[1152]{0:T(1024)}) all-reduce(f32[2,576]{1,0:T(2,128)} %pad_maximum_fusion.5, bf16[1152]{0:T(1024)(128)(2,1)S(1)} %get-tuple-element.57, f32[2304]{0:T(1024)} %get-tuple-element.80, ...), channel_id=1, replica_groups=mesh['dp'=16,'tensor'=2] {'dp'}, use_global_device_ids=true, to_apply=%region_28.29 | all-reduce | flops 5760 | bytes 43776 | tf_op jit(solution)/shard_map/psum | solution.py:277
  984.5 18.4 %all-gather.1 = bf16[16,1,6912]{2,1,0:T(2,128)(2,1)S(1)} all-gather(bf16[1,1,6912]{2,1,0:T(2,128)(2,1)S(1)} %bitcast.239), channel_id=1, replica_groups=mesh['dp'=16,'tensor'=2] {'dp'}, dimensions={0}, use_global_device_ids=true | all-gather | bytes 235008 | tf_op jit(solution)/shard_map/all_gather | solution.py:253
  1006.0 10.3 %fusion.89 = f32[1,1152]{1,0:T(1,128)} fusion(bf16[1152,6912]{1,0:T(8,128)(2,1)} %all-gather.12.cloned.1.call-done, bf16[1,6912]{1,0:T(2,128)(2,1)S(1)} %get-tuple-element.56, bf16[1,1152]{1,0:T(2,128)(2,1)S(1)} %copy-done.48), kind=kOutput, calls=%fused_computation.145 | convolution fusion | flops 15936768 | bytes 15945984 | tf_op jit(solution)/shard_map/le,de->ld/dot_general | solution.py:249
  (260 shorter events, 82.2 us)
Async XLA Ops:
  7.2 127.3 %copy-start.46 = (bf16[1,1152]{1,0:T(2,128)(2,1)S(1)}, bf16[1,1152]{1,0:T(2,128)(2,1)}, u32[]{:S(2)}) copy-start(bf16[1,1152]{1,0:T(2,128)(2,1)} %param.14) | copy-start | bytes 6916
  7.2 127.3 %all-gather.12.cloned.1.call-start = ((), (), s32[]{:S(2)}) async-start(), calls=%async_computation.8 | async-start | bytes 16920576 | tf_op jit(solution)/shard_map/all_gather | solution.py:106
  7.9 178.7 %all-gather.16.cloned.1.call-start = ((), (), s32[]{:S(2)}) async-start(), calls=%async_computation.10 | async-start | bytes 4700160 | tf_op jit(solution)/shard_map/all_gather | solution.py:107
  8.7 214.7 %all-gather.14.cloned.1.call-start = ((), (), s32[]{:S(2)}) async-start(), calls=%async_computation.9 | async-start | bytes 3538944 | tf_op jit(solution)/shard_map/all_gather | solution.py:126
  10.2 132.7 %copy-start.38 = (f32[512]{0:T(512)}, f32[512]{0:T(512)S(1)}, u32[]{:S(2)}) copy-start(f32[512]{0:T(512)S(1)} %broadcast_multiply_fusion.1) | copy-start | bytes 6148
  10.7 123.8 %copy-start.53 = (f32[512]{0:T(512)}, f32[512]{0:T(512)S(1)}, u32[]{:S(2)}) copy-start(f32[512]{0:T(512)S(1)} %fusion.42) | copy-start | bytes 6148
  10.7 132.2 %copy-start.43 = (f32[512]{0:T(512)}, f32[512]{0:T(512)S(1)}, u32[]{:S(2)}) copy-start(f32[512]{0:T(512)S(1)} %fusion.96) | copy-start | bytes 6148
  10.7 131.5 %copy-start.58 = (bf16[6912]{0:T(1024)(128)(2,1)S(1)}, bf16[6912]{0:T(1024)(128)(2,1)}, u32[]{:S(2)}) copy-start(bf16[6912]{0:T(1024)(128)(2,1)} %param.16) | copy-start | bytes 41476
  142.9 50.2 %copy-start.31 = (f32[1152]{0:T(1024)}, f32[1152]{0:T(1024)S(1)}, u32[]{:S(2)}) copy-start(f32[1152]{0:T(1024)S(1)} %get-tuple-element.50) | copy-start | bytes 13828
  142.9 427.8 %copy-start.25 = (f32[1152]{0:T(1024)}, f32[1152]{0:T(1024)S(1)}, u32[]{:S(2)}) copy-start(f32[1152]{0:T(1024)S(1)} %get-tuple-element.51) | copy-start | bytes 13828
  144.5 127.9 %all-gather.18.cloned.1.call-start = ((), (), s32[]{:S(2)}) async-start(), calls=%async_computation.11 | async-start | bytes 1566720 | tf_op jit(solution)/shard_map/all_gather | solution.py:108
  145.0 167.5 %reduce-scatter.13.cloned.1.call-start = ((), (), s32[]{:S(2)}) async-start(), calls=%async_computation.12 | async-start | bytes 3538944 | tf_op jit(solution)/shard_map/reduce_scatter | solution.py:148
  231.0 36.0 %copy-start.7 = (bf16[1024,3,576]{0,2,1:T(8,128)(2,1)}, bf16[1024,3,576]{0,2,1:T(8,128)(2,1)S(1)}, u32[]{:S(2)}) copy-start(bf16[1024,3,576]{0,2,1:T(8,128)(2,1)S(1)} %add_convert_fusion) | copy-start | bytes 10616836
  239.1 16.1 %copy-start.32 = (f32[8,512]{1,0:T(8,128)}, f32[8,512]{1,0:T(8,128)S(1)}, u32[]{:S(2)}) copy-start(f32[8,512]{1,0:T(8,128)S(1)} %get-tuple-element.72) | copy-start | bytes 49156
  241.6 25.4 %copy-start = (f32[8,512,1024]{2,1,0:T(8,128)}, f32[8,512,1024]{2,1,0:T(8,128)S(1)}, u32[]{:S(2)}) copy-start(f32[8,512,1024]{2,1,0:T(8,128)S(1)} %get-tuple-element.75) | copy-start | bytes 50331652
  241.7 25.4 %copy-start.34 = (f32[8,512]{1,0:T(8,128)}, f32[8,512]{1,0:T(8,128)S(1)}, u32[]{:S(2)}) copy-start(f32[8,512]{1,0:T(8,128)S(1)} %get-tuple-element.74) | copy-start | bytes 49156
  277.6 93.6 %all-gather.22.cloned.1.call-start = ((), (), s32[]{:S(2)}) async-start(), calls=%async_computation.14 | async-start | bytes 5640192 | tf_op jit(solution)/shard_map/all_gather | solution.py:109
  278.2 129.9 %all-gather.20.cloned.1.call-start = ((), (), s32[]{:S(2)}) async-start(), calls=%async_computation.13 | async-start | bytes 3538944 | tf_op jit(solution)/shard_map/all_gather | solution.py:159
  278.3 291.3 %copy-start.27 = (f32[1152]{0:T(1024)}, f32[1152]{0:T(1024)S(1)}, u32[]{:S(2)}) copy-start(f32[1152]{0:T(1024)S(1)} %convert_element_type.196) | copy-start | bytes 13828
  317.6 149.3 %all-gather.24.cloned.1.call-start = ((), (), s32[]{:S(2)}) async-start(), calls=%async_computation.15 | async-start | bytes 5640192 | tf_op jit(solution)/shard_map/all_gather | solution.py:110
  318.4 185.4 %all-gather.26.cloned.1.call-start = ((), (), s32[]{:S(2)}) async-start(), calls=%async_computation.17 | async-start | bytes 3538944 | tf_op jit(solution)/shard_map/all_gather | solution.py:181
  320.4 245.9 %reduce-scatter.17.cloned.1.call-start = ((), (), s32[]{:S(2)}) async-start(), calls=%async_computation.18 | async-start | bytes 3538944 | tf_op jit(solution)/shard_map/reduce_scatter | solution.py:193
  531.4 77.8 %all-gather.28.cloned.1.call-start = ((), (), s32[]{:S(2)}) async-start(), calls=%async_computation.19 | async-start | bytes 3538944 | tf_op jit(solution)/shard_map/all_gather | solution.py:210
  572.9 230.2 %reduce-scatter.23.cloned.1.call-start = ((), (), s32[]{:S(2)}) async-start(), calls=%async_computation.22 | async-start | bytes 5640192 | tf_op jit(solution)/shard_map/reduce_scatter | solution.py:273
  584.6 220.4 %reduce-scatter.21.cloned.1.call-start = ((), (), s32[]{:S(2)}) async-start(), calls=%async_computation.21 | async-start | bytes 5640192 | tf_op jit(solution)/shard_map/reduce_scatter | solution.py:270
  596.0 13.2 %copy-start.66 = (bf16[576,1152]{0,1:T(8,128)(2,1)S(1)}, bf16[576,1152]{0,1:T(8,128)(2,1)}, u32[]{:S(2)}) copy-start(bf16[576,1152]{0,1:T(8,128)(2,1)} %all-gather.18.cloned.1.call-done) | copy-start | bytes 3981316
  596.0 241.4 %reduce-scatter.27.cloned.1.call-start = ((), (), s32[]{:S(2)}) async-start(), calls=%async_computation.24 | async-start | bytes 1566720
  613.5 15.2 %copy-start.17 = (bf16[512,576]{0,1:T(8,128)(2,1)}, bf16[512,576]{0,1:T(8,128)(2,1)S(1)}, u32[]{:S(2)}) copy-start(bf16[512,576]{0,1:T(8,128)(2,1)S(1)} %get-tuple-element.66) | copy-start | bytes 1769476
  613.5 15.2 %slice-start = ((s8[16777216]{0:T(1024)(128)(4,1)}), s8[4194304]{0:T(1024)(128)(4,1)S(1)}, s32[]{:S(2)}) async-start(s8[16777216]{0:T(1024)(128)(4,1)} %bitcast.212), calls=%async_computation.25 | async-start | bytes 8388608
  613.5 15.2 %slice-start.1 = ((s8[16777216]{0:T(1024)(128)(4,1)}), s8[4194304]{0:T(1024)(128)(4,1)S(1)}, s32[]{:S(2)}) async-start(s8[16777216]{0:T(1024)(128)(4,1)} %bitcast.212), calls=%async_computation.26 | async-start | bytes 8388608
  613.5 16.8 %slice-start.2 = ((s8[16777216]{0:T(1024)(128)(4,1)}), s8[4194304]{0:T(1024)(128)(4,1)S(1)}, s32[]{:S(2)}) async-start(s8[16777216]{0:T(1024)(128)(4,1)} %bitcast.212), calls=%async_computation.27 | async-start | bytes 8388608
  613.5 18.2 %slice-start.3 = ((s8[16777216]{0:T(1024)(128)(4,1)}), s8[4194304]{0:T(1024)(128)(4,1)S(1)}, s32[]{:S(2)}) async-start(s8[16777216]{0:T(1024)(128)(4,1)} %bitcast.212), calls=%async_computation.28 | async-start | bytes 8388608
  631.7 11.0 %copy-start.68 = (bf16[8,72,512]{2,1,0:T(8,128)(2,1)S(1)}, bf16[8,72,512]{2,1,0:T(8,128)(2,1)}, u32[]{:S(2)}) copy-start(bf16[8,72,512]{2,1,0:T(8,128)(2,1)} %copy-done.67) | copy-start | bytes 1769476
  631.7 11.0 %copy-start.70 = (bf16[8,72,512]{2,1,0:T(8,128)(2,1)S(1)}, bf16[8,72,512]{2,1,0:T(8,128)(2,1)}, u32[]{:S(2)}) copy-start(bf16[8,72,512]{2,1,0:T(8,128)(2,1)} %copy-done.69) | copy-start | bytes 1769476
  668.1 28.3 %slice-start.4 = ((s8[16777216]{0:T(1024)(128)(4,1)}), s8[4194304]{0:T(1024)(128)(4,1)S(1)}, s32[]{:S(2)}) async-start(s8[16777216]{0:T(1024)(128)(4,1)} %bitcast.214), calls=%async_computation.29 | async-start | bytes 8388608
  668.1 28.3 %slice-start.5 = ((s8[16777216]{0:T(1024)(128)(4,1)}), s8[4194304]{0:T(1024)(128)(4,1)S(1)}, s32[]{:S(2)}) async-start(s8[16777216]{0:T(1024)(128)(4,1)} %bitcast.214), calls=%async_computation.30 | async-start | bytes 8388608
  668.1 28.4 %slice-start.6 = ((s8[16777216]{0:T(1024)(128)(4,1)}), s8[4194304]{0:T(1024)(128)(4,1)S(1)}, s32[]{:S(2)}) async-start(s8[16777216]{0:T(1024)(128)(4,1)} %bitcast.214), calls=%async_computation.31 | async-start | bytes 8388608
  700.8 172.4 %reduce-scatter.19.cloned.1.call-start = ((), (), s32[]{:S(2)}) async-start(), calls=%async_computation.20 | async-start | bytes 3538944 | tf_op jit(solution)/shard_map/reduce_scatter | solution.py:228
  718.7 191.5 %reduce-scatter.15.cloned.1.call-start = ((), (), s32[]{:S(2)}) async-start(), calls=%async_computation.16 | async-start | bytes 3538944 | tf_op jit(solution)/shard_map/reduce_scatter | solution.py:168
  733.2 283.2 %reduce-scatter.25.cloned.1.call-start = ((), (), s32[]{:S(2)}) async-start(), calls=%async_computation.23 | async-start | bytes 4386816
  773.0 26.2 %copy-start.16 = (bf16[512,1152]{1,0:T(8,128)(2,1)S(1)}, bf16[512,1152]{1,0:T(8,128)(2,1)}, u32[]{:S(2)}) copy-start(bf16[512,1152]{1,0:T(8,128)(2,1)} %reduce-scatter.17.cloned.1.call-done) | copy-start | bytes 3538948
  773.0 27.0 %copy-start.57 = (bf16[1152]{0:T(1024)(128)(2,1)S(1)}, bf16[1152]{0:T(1024)(128)(2,1)}, u32[]{:S(2)}) copy-start(bf16[1152]{0:T(1024)(128)(2,1)} %get-tuple-element.40) | copy-start | bytes 6916
  773.0 27.6 %copy-start.13 = (bf16[8,72,1024]{2,1,0:T(8,128)(2,1)S(1)}, bf16[8,72,1024]{2,1,0:T(8,128)(2,1)}, u32[]{:S(2)}) copy-start(bf16[8,72,1024]{2,1,0:T(8,128)(2,1)} %fusion.67) | copy-start | bytes 3538948
  802.5 72.8 %copy-start.2 = (bf16[512,1,1152]{2,0,1:T(8,128)(2,1)S(1)}, bf16[512,1,1152]{2,0,1:T(8,128)(2,1)}, u32[]{:S(2)}) copy-start(bf16[512,1,1152]{2,0,1:T(8,128)(2,1)} %param.13) | copy-start | bytes 3538948
  875.4 34.8 %copy-start.6 = (bf16[512,1152]{1,0:T(8,128)(2,1)S(1)}, bf16[512,1152]{1,0:T(8,128)(2,1)}, u32[]{:S(2)}) copy-start(bf16[512,1152]{1,0:T(8,128)(2,1)} %reduce-scatter.13.cloned.1.call-done) | copy-start | bytes 3538948
  875.4 34.8 %copy-start.26 = (f32[1152]{0:T(1024)S(1)}, f32[1152]{0:T(1024)}, u32[]{:S(2)}) copy-start(f32[1152]{0:T(1024)} %copy-done.25) | copy-start | bytes 13828
  875.4 34.8 %copy-start.28 = (f32[1152]{0:T(1024)S(1)}, f32[1152]{0:T(1024)}, u32[]{:S(2)}) copy-start(f32[1152]{0:T(1024)} %copy-done.27) | copy-start | bytes 13828
  915.2 90.8 %copy-start.48 = (bf16[1,1152]{1,0:T(2,128)(2,1)S(1)}, bf16[1,1152]{1,0:T(2,128)(2,1)}, u32[]{:S(2)}) copy-start(bf16[1,1152]{1,0:T(2,128)(2,1)} %param.14) | copy-start | bytes 6916
  (49 other events, 158.5 us)
Sparse Core Ops, SparseCore 0:
  10.2 124.2 all-gather.11
  136.7 49.9 all-gather.15
  188.7 34.5 all-gather.13
  225.3 39.3 all-gather.17
  277.7 34.7 reduce-scatter.12
  314.8 56.3 all-gather.21
  373.4 34.6 all-gather.19
  410.5 56.3 all-gather.23
  469.1 34.6 all-gather.25
  531.5 34.6 reduce-scatter.16
  573.0 36.0 all-gather.27
  613.0 79.7 reduce-scatter.22
  696.9 78.7 reduce-scatter.20
  779.8 57.5 reduce-scatter.26
  839.5 33.6 reduce-scatter.18
  875.4 34.6 reduce-scatter.14
  913.9 72.8 reduce-scatter.24
where the time goes:
time: 1030 us
  waiting for transfers between devices  543 us (53%)
  matrix products  207 us (20%)
  blocking collectives  108 us (10%)
  other arithmetic  87 us (8%)
  local copies, waits for them, and re-layouts  62.4 us (6%)
  between operations  14.9 us (1%)
    all_gather x1, waiting for transfers between devices, on_device(): lax.all_gather(mod_weight, 'dp', axis=0, tiled=True)  124 us
    psum x1, blocking collectives, on_device(): lax.psum((qkv_bias_grad, proj_bias_grad, fc1_bias_grad, fc2_bias_grad), '...  60.7 us
    unnamed x164, local copies, waits for them, and re-layouts  51 us
    all_gather x1, waiting for transfers between devices, on_device(): lax.all_gather(first_hidden_weight, 'dp', axis=0, tiled=True)  49.5 us
    all_gather x1, waiting for transfers between devices, on_device(): lax.all_gather(second_hidden_weight, 'dp', axis=1, tiled=True)  47.1 us
    all_gather x1, waiting for transfers between devices, on_device(): lax.all_gather(query_key_value_weight, 'dp', axis=0, tiled=True)  40.8 us
    all_gather x1, waiting for transfers between devices, on_device(): lax.all_gather(grad_m_low, 'tensor', axis=0, tiled=True)  36.9 us
    all_gather x1, waiting for transfers between devices, on_device(): lax.all_gather(feedforward_normalized.astype(jnp.bfloat16), 'tensor', axi...  36.9 us
  transfers between devices with their start and end apart: 17, of which 13 were waited for; matrix products, arithmetic and copies ran while one was open for 29% of the time, Pallas kernels for 0%

commit v1 on v0

--- a/solution.py
+++ b/solution.py
@@ -4,6 +4,24 @@
 from jax.sharding import PartitionSpec as P
 
 HEADS = 16
+
+
+def gather_around(value, axis, dim):
+    ways, here, step = (lax.axis_size(axis), lax.axis_index(axis), value.shape[dim])
+    shape = [n * ways if d == dim else n for d, n in enumerate(value.shape)]
+    full = lax.dynamic_update_slice_in_dim(
+        jnp.zeros(shape, value.dtype), value, here * step, axis=dim
+    )
+    going_up = going_down = value
+    for far in range(1, ways // 2 + 1):
+        going_up = lax.ppermute(going_up, axis, [(d, (d + 1) % ways) for d in range(ways)])
+        full = lax.dynamic_update_slice_in_dim(full, going_up, (here - far) % ways * step, axis=dim)
+        if 2 * far < ways:
+            going_down = lax.ppermute(going_down, axis, [(d, (d - 1) % ways) for d in range(ways)])
+            full = lax.dynamic_update_slice_in_dim(
+                full, going_down, (here + far) % ways * step, axis=dim
+            )
+    return full
 
 
 def modulate(hidden, shifts, scales):
@@ -106,7 +124,7 @@
         lax.all_gather(mod_weight, "dp", axis=0, tiled=True),
         lax.all_gather(query_key_value_weight, "dp", axis=0, tiled=True),
         lax.all_gather(attention_out_weight, "dp", axis=1, tiled=True),
-        lax.all_gather(first_hidden_weight, "dp", axis=0, tiled=True),
+        gather_around(first_hidden_weight, "dp", 0),
         lax.all_gather(second_hidden_weight, "dp", axis=1, tiled=True),
     )
     seq_local, latents, width = tokens.shape

time: 1030 us -> 988 us (0.959)
  waiting for transfers between devices: 543 us -> 441 us
  starting transfers between devices: 1.62 us -> 33.2 us
  local copies, waits for them, and re-layouts: 62.4 us -> 77.5 us
    all_gather x1 -> x0, waiting for transfers between devices: 49.5 us -> none  [on_device(): lax.all_gather(first_hidden_weight, 'dp', axis=0, tiled=True)]
    all_gather x1, waiting for transfers between devices: 47.1 us -> 0.01 us  [on_device(): lax.all_gather(second_hidden_weight, 'dp', axis=1, tiled=True)]
    ppermute x0 -> x15, waiting for transfers between devices: none -> 38.4 us  [the longest x8 19.6 us: gather_around(): lax.ppermute(going_up, axis, [(d, (d + 1) % ways) for d in range(ways)])]
    all_gather x1, waiting for transfers between devices: 36.9 us -> 0.01 us  [on_device(): lax.all_gather(feedforward_normalized.astype(jnp.bfloat16), 'tensor', axi...]
    ppermute x0 -> x15, starting transfers between devices: none -> 31.7 us  [the longest x7 31.6 us: gather_around(): lax.ppermute(going_down, axis, [(d, (d - 1) % ways) for d in range(ways)])]
    dynamic_update_slice x0 -> x16, local copies, waits for them, and re-layouts: none -> 19 us  [the longest x8 8.98 us: gather_around(): lax.dynamic_update_slice_in_dim(full, going_up, (here - far) % ways * ste...]
    unnamed x164 -> x156, local copies, waits for them, and re-layouts: 51 us -> 43.6 us
    unnamed x19 -> x18, waiting for transfers between devices: 33.8 us -> 30.2 us
  transfers between devices with their start and end apart: 17 -> 31, of which waited for: 13 -> 19; matrix products, arithmetic and copies ran while one was open for 29% -> 33% of each run, Pallas kernels for 0% -> 0%
where the time goes in v1:
time: 988 us; the launch traced here: 982 us
  waiting for transfers between devices  441 us (45%)
  matrix products  214 us (22%)
  blocking collectives  108 us (11%)
  other arithmetic  93.4 us (9%)
  local copies, waits for them, and re-layouts  77.5 us (8%)
  starting transfers between devices  33.2 us (3%)
  between operations  14.9 us (2%)
    all_gather x1, waiting for transfers between devices, on_device(): lax.all_gather(mod_weight, 'dp', axis=0, tiled=True)  122 us
    psum x1, blocking collectives, on_device(): lax.psum((qkv_bias_grad, proj_bias_grad, fc1_bias_grad, fc2_bias_grad), '...  60.8 us
    unnamed x156, local copies, waits for them, and re-layouts  43.6 us
    all_gather x1, waiting for transfers between devices, on_device(): lax.all_gather(query_key_value_weight, 'dp', axis=0, tiled=True)  40.8 us
    reduce_scatter x1, waiting for transfers between devices, on_device(): lax.psum_scatter(jnp.dot(attended_rows, w_proj, preferred_element_type=jn...  34.8 us
    all_gather x1, waiting for transfers between devices, on_device(): lax.all_gather(grad_m_low, 'tensor', axis=0, tiled=True)  34.6 us
    reduce_scatter x1, waiting for transfers between devices, on_device(): lax.psum_scatter(jnp.einsum('rf,df->rd', pre_grad, w_fc1, preferred_eleme...  34.4 us
    reduce_scatter x1, waiting for transfers between devices, on_device(): lax.psum_scatter(jnp.einsum('rc,dc->rd', qkv_grad_rows, qkv_flat, preferr...  34.2 us
  transfers between devices with their start and end apart: 31, of which 19 were waited for; matrix products, arithmetic and copies ran while one was open for 33% of the time, Pallas kernels for 0%

profile of v1, /device:TPU:0, one launch (start us, length us, event | category | flops | bytes accessed | tf_op | source)
XLA Modules:
  0.0 982.4 jit_solution(10997163675689833448)
XLA Ops:
  12.0 122.4 %all-gather.11.cloned.1.call-done = bf16[1152,6912]{1,0:T(8,128)(2,1)} async-done(((bf16[72,6912]{1,0:T(8,128)(2,1)}), bf16[1152,6912]{1,0:T(8,128)(2,1)}) %all-gather.11.cloned.1.call-update) | async-done | bytes 15925264 | tf_op jit(solution)/shard_map/all_gather | solution.py:124
  134.5 7.7 convolution_reduce_fusion
  145.8 40.8 %all-gather.15.cloned.1.call-done = bf16[1152,3,576]{2,0,1:T(8,128)(2,1)} async-done(((bf16[72,3,576]{2,0,1:T(8,128)(2,1)}), bf16[1152,3,576]{2,0,1:T(8,128)(2,1)}) %all-gather.15.cloned.1.call-update) | async-done | bytes 3981328 | tf_op jit(solution)/shard_map/all_gather | solution.py:125
  186.6 6.6 copy.29
  193.2 30.1 %all-gather.13.cloned.1.call-done = bf16[1024,1,1152]{2,0,1:T(8,128)(2,1)} async-done(((bf16[512,1,1152]{2,0,1:T(8,128)(2,1)}), bf16[1024,1,1152]{2,0,1:T(8,128)(2,1)}) %all-gather.13.cloned.1.call-update) | async-done | bytes 2359312 | tf_op jit(solution)/shard_map/all_gather | solution.py:144
  223.3 7.6 add_convert_fusion
  231.0 8.2 multiply_reduce_fusion.2
  241.7 13.6 %fusion.1 = f32[8,512]{1,0:T(8,128)S(1)} fusion(f32[8,512,1024]{2,1,0:T(8,128)} %get-tuple-element.73, f32[8,512]{1,0:T(8,128)S(1)} %get-tuple-element.72), kind=kLoop, calls=%fused_computation.11 | loop fusion | flops 12578816 | bytes 16809984 | tf_op jit(solution)/shard_map/while/body/eval_jaxpr/reduce_sum | solution.py:54
  255.3 7.9 fusion.75
  272.4 5.2 convolution_convert_fusion.6
  277.7 34.8 %reduce-scatter.13.cloned.1.call-done = bf16[512,1152]{1,0:T(8,128)(2,1)} async-done(((bf16[1024,1152]{1,0:T(8,128)(2,1)}), bf16[512,1152]{1,0:T(8,128)(2,1)}) %reduce-scatter.13.cloned.1.call-update) | async-done | bytes 1179664 | tf_op jit(solution)/shard_map/reduce_scatter | solution.py:166
  346.7 4.7 collective-permute-start.7
  356.1 4.7 collective-permute-start.9
  371.7 8.0 collective-permute-done.11
  379.8 4.7 collective-permute-start.13
  390.4 9.4 collective-permute-done.12
  403.2 9.0 collective-permute-done.14
  412.9 11.8 %fusion.57 = f32[1024,2304]{1,0:T(8,128)} fusion(bf16[1152,2304]{1,0:T(8,128)(2,1)} %constant_dynamic-update-slice_fusion, bf16[1024,1,1152]{2,0,1:T(8,128)(2,1)} %all-gather.19.cloned.1.call-done), kind=kOutput, calls=%fused_computation.98 | convolution fusion | flops 5435817984 | bytes 17104896 | tf_op jit(solution)/shard_map/dot_general | solution.py:181
  424.8 34.6 %all-gather.23.cloned.1.call-done = bf16[1024,1,1152]{2,0,1:T(8,128)(2,1)} async-done(((bf16[512,1,1152]{2,0,1:T(8,128)(2,1)}), bf16[1024,1,1152]{2,0,1:T(8,128)(2,1)}) %all-gather.23.cloned.1.call-update) | async-done | bytes 2359312 | tf_op jit(solution)/shard_map/all_gather | solution.py:199
  459.3 15.4 %convert_reduce_fusion = (f32[2304]{0:T(1024)}, bf16[1024,2304]{1,0:T(8,128)(2,1)S(1)}) fusion(f32[1024,2304]{1,0:T(8,128)} %fusion.57, f32[2304]{0:T(1024)} %convert_element_type.198, bf16[2304,1152]{0,1:T(8,128)(2,1)} %all-gather.21.cloned.1.call-done, bf16[1024,1,1152]{2,0,1:T(8,128)(2,1)} %all-gather.23.cloned.1.call-done), kind=kOutput, calls=%fused_computation.27 | convolution fusion | flops 5490079744 | bytes 21841920 | tf_op jit(solution)/shard_map/rd,fd->rf/dot_general | solution.py:206
  476.9 10.0 %convolution_convert_fusion.3 = bf16[1024,1152]{1,0:T(8,128)(2,1)} fusion(bf16[1024,2304]{1,0:T(8,128)(2,1)S(1)} %get-tuple-element.81, bf16[1152,2304]{1,0:T(8,128)(2,1)} %constant_dynamic-update-slice_fusion), kind=kOutput, calls=%fused_computation.44 | convolution fusion | flops 5436997632 | bytes 12386304 | tf_op jit(solution)/shard_map/rf,df->rd/dot_general | solution.py:212
  487.4 34.4 %reduce-scatter.17.cloned.1.call-done = bf16[512,1152]{1,0:T(8,128)(2,1)} async-done(((bf16[1024,1152]{1,0:T(8,128)(2,1)}), bf16[512,1152]{1,0:T(8,128)(2,1)}) %reduce-scatter.17.cloned.1.call-update) | async-done | bytes 1179664 | tf_op jit(solution)/shard_map/reduce_scatter | solution.py:211
  530.0 10.9 %convolution_convert_fusion = bf16[2304,1152]{0,1:T(8,128)(2,1)} fusion(bf16[1024,1,1152]{2,0,1:T(8,128)(2,1)S(1)} %copy-done.22, f32[1024,2304]{1,0:T(8,128)} %fusion.57, f32[2304]{0:T(1024)} %convert_element_type.198), kind=kOutput, calls=%fused_computation.16 | convolution fusion | flops 5462065152 | bytes 17114112 | tf_op jit(solution)/shard_map/rf,rd->fd/dot_general | solution.py:203
  542.6 9.7 convolution_convert_fusion.1
  552.4 13.8 %all-gather.25.cloned.1.call-done = bf16[1024,1,1152]{2,0,1:T(8,128)(2,1)} async-done(((bf16[512,1,1152]{2,0,1:T(8,128)(2,1)}), bf16[1024,1,1152]{2,0,1:T(8,128)(2,1)}) %all-gather.25.cloned.1.call-update) | async-done | bytes 2359312 | tf_op jit(solution)/shard_map/all_gather | solution.py:228
  570.5 15.2 %multiply_reduce_fusion.1 = (f32[8,512]{1,0:T(8,128)S(1)}, f32[8,512,1024]{2,1,0:T(8,128)}) fusion(f32[8,512,1024]{2,1,0:T(8,128)} %copy-done, f32[8,512]{1,0:T(8,128)S(1)} %log_add_fusion.1, bf16[512,8,72]{0,2,1:T(8,128)(2,1)S(1)} %bitcast.230, bf16[1024,3,8,72]{0,3,2,1:T(8,128)(2,1)} %bitcast.220), kind=kOutput, calls=%fused_computation.4 | convolution fusion | flops 620752896 | bytes 35356672 | tf_op jit(solution)/shard_map/while/body/eval_jaxpr/qhe,khe->hqk/dot_general | solution.py:84
  588.7 11.0 %multiply_convert_fusion.1 = bf16[8,512,1024]{2,1,0:T(8,128)(2,1)} fusion(f32[8,512,1024]{2,1,0:T(8,128)} %get-tuple-element.77, f32[8,512,1024]{2,1,0:T(8,128)S(1)} %bitcast.213, f32[8,512]{1,0:T(8,128)S(1)} %get-tuple-element.76, f32[8,512]{1,0:T(8,128)S(1)} %log_add_fusion.1), kind=kLoop, calls=%fused_computation.3 | loop fusion | flops 20971520 | bytes 41975808 | tf_op jit(solution)/shard_map/while/body/eval_jaxpr/convert_element_type | solution.py:88
  603.0 6.5 fusion.82
  613.0 11.5 %multiply_reduce_fusion = (f32[8,512]{1,0:T(8,128)S(1)}, f32[8,512,1024]{2,1,0:T(8,128)}) fusion(f32[8,512,1024]{2,1,0:T(8,128)} %get-tuple-element.73, f32[8,512]{1,0:T(8,128)S(1)} %copy-done.27, bf16[512,8,72]{0,2,1:T(8,128)(2,1)S(1)} %bitcast.232, bf16[1024,3,8,72]{0,3,2,1:T(8,128)(2,1)S(1)} %bitcast.223), kind=kOutput, calls=%fused_computation.1 | convolution fusion | flops 620752896 | bytes 35356672 | tf_op jit(solution)/shard_map/while/body/eval_jaxpr/qhe,khe->hqk/dot_general | solution.py:84
  624.5 16.3 %multiply_convert_fusion = bf16[8,512,1024]{2,1,0:T(8,128)(2,1)} fusion(f32[8,512,1024]{2,1,0:T(8,128)} %get-tuple-element.79, f32[8,512,1024]{2,1,0:T(8,128)} %get-tuple-element.73, f32[8,512]{1,0:T(8,128)S(1)} %get-tuple-element.78, f32[8,512]{1,0:T(8,128)S(1)} %copy-done.27), kind=kLoop, calls=%fused_computation | loop fusion | flops 20971520 | bytes 41975808 | tf_op jit(solution)/shard_map/while/body/eval_jaxpr/convert_element_type | solution.py:88
  640.9 7.1 fusion.74
  648.0 9.0 fusion.11
  657.1 5.7 fusion.67
  665.7 5.6 add_multiply_fusion
  674.0 6.3 convolution_convert_fusion.5
  680.4 14.5 %convolution_convert_fusion.4 = bf16[1024,1152]{1,0:T(8,128)(2,1)} fusion(bf16[2304,1152]{0,1:T(8,128)(2,1)} %all-gather.21.cloned.1.call-done, f32[1024,2304]{1,0:T(8,128)} %fusion.57, f32[2304]{0:T(1024)S(1)} %copy-done.55), kind=kOutput, calls=%fused_computation.45 | convolution fusion | flops 5460590592 | bytes 17114112 | tf_op jit(solution)/shard_map/dot_general | solution.py:187
  694.9 7.9 convolution_convert_fusion.2
  702.8 18.2 %copy.34 = bf16[1152,3,576]{2,1,0:T(4,128)(2,1)} copy(bf16[1152,3,576]{2,0,1:T(8,128)(2,1)S(1)} %convolution_convert_fusion.2) | data formatting | bytes 7962624
  721.1 12.3 %reshape.346 = bf16[1152,1728]{1,0:T(8,128)(2,1)} reshape(bf16[1152,3,576]{2,1,0:T(4,128)(2,1)} %copy.34) | data formatting | bytes 7962624
  734.7 21.5 %all-gather = bf16[16,1,1152]{2,1,0:T(2,128)(2,1)S(1)} all-gather(bf16[1,1,1152]{2,1,0:T(2,128)(2,1)S(1)} %convert_bitcast_fusion.2), channel_id=1, replica_groups=mesh['dp'=16,'tensor'=2] {'dp'}, dimensions={0}, use_global_device_ids=true | all-gather | bytes 39168 | tf_op jit(solution)/shard_map/all_gather | solution.py:270
  767.3 27.4 %reduce-scatter.27.cloned.1.call-done = bf16[576,72]{0,1:T(8,128)(2,1)} async-done(((bf16[576,1152]{0,1:T(8,128)(2,1)}), bf16[576,72]{0,1:T(8,128)(2,1)}) %reduce-scatter.27.cloned.1.call-update) | async-done | bytes 82960
  796.2 34.2 %reduce-scatter.19.cloned.1.call-done = bf16[512,1152]{1,0:T(8,128)(2,1)} async-done(((bf16[1024,1152]{1,0:T(8,128)(2,1)}), bf16[512,1152]{1,0:T(8,128)(2,1)}) %reduce-scatter.19.cloned.1.call-update) | async-done | bytes 1179664 | tf_op jit(solution)/shard_map/reduce_scatter | solution.py:246
  840.2 27.2 %reduce-scatter.15.cloned.1.call-done = bf16[512,1152]{1,0:T(8,128)(2,1)} async-done(((bf16[1024,1152]{1,0:T(8,128)(2,1)}), bf16[512,1152]{1,0:T(8,128)(2,1)}) %reduce-scatter.15.cloned.1.call-update) | async-done | bytes 1179664 | tf_op jit(solution)/shard_map/reduce_scatter | solution.py:186
  867.4 5.1 fusion.45
  873.3 7.8 all-reduce.2
  881.1 60.8 %all-reduce.1 = (f32[2,576]{1,0:T(2,128)}, f32[1152]{0:T(1024)}, f32[2304]{0:T(1024)}, f32[1152]{0:T(1024)}) all-reduce(f32[2,576]{1,0:T(2,128)} %pad_maximum_fusion.5, bf16[1152]{0:T(1024)(128)(2,1)S(1)} %get-tuple-element.57, f32[2304]{0:T(1024)} %get-tuple-element.80, ...), channel_id=1, replica_groups=mesh['dp'=16,'tensor'=2] {'dp'}, use_global_device_ids=true, to_apply=%region_28.29 | all-reduce | flops 5760 | bytes 43776 | tf_op jit(solution)/shard_map/psum | solution.py:295
  941.9 18.4 %all-gather.1 = bf16[16,1,6912]{2,1,0:T(2,128)(2,1)S(1)} all-gather(bf16[1,1,6912]{2,1,0:T(2,128)(2,1)S(1)} %bitcast.239), channel_id=1, replica_groups=mesh['dp'=16,'tensor'=2] {'dp'}, dimensions={0}, use_global_device_ids=true | all-gather | bytes 235008 | tf_op jit(solution)/shard_map/all_gather | solution.py:271
  963.4 10.3 %fusion.89 = f32[1,1152]{1,0:T(1,128)} fusion(bf16[1152,6912]{1,0:T(8,128)(2,1)} %all-gather.11.cloned.1.call-done, bf16[1,6912]{1,0:T(2,128)(2,1)S(1)} %get-tuple-element.56, bf16[1,1152]{1,0:T(2,128)(2,1)} %param.14), kind=kOutput, calls=%fused_computation.145 | convolution fusion | flops 15936768 | bytes 15945984 | tf_op jit(solution)/shard_map/le,de->ld/dot_general | solution.py:267
  (296 shorter events, 141.6 us)
Async XLA Ops:
  7.2 127.3 %copy-start.44 = (bf16[1,1152]{1,0:T(2,128)(2,1)S(1)}, bf16[1,1152]{1,0:T(2,128)(2,1)}, u32[]{:S(2)}) copy-start(bf16[1,1152]{1,0:T(2,128)(2,1)} %param.14) | copy-start | bytes 6916
  7.2 127.3 %all-gather.11.cloned.1.call-start = ((), (), s32[]{:S(2)}) async-start(), calls=%async_computation.8 | async-start | bytes 16920576 | tf_op jit(solution)/shard_map/all_gather | solution.py:124
  7.9 178.7 %all-gather.15.cloned.1.call-start = ((), (), s32[]{:S(2)}) async-start(), calls=%async_computation.10 | async-start | bytes 4700160 | tf_op jit(solution)/shard_map/all_gather | solution.py:125
  8.7 214.7 %all-gather.13.cloned.1.call-start = ((), (), s32[]{:S(2)}) async-start(), calls=%async_computation.9 | async-start | bytes 3538944 | tf_op jit(solution)/shard_map/all_gather | solution.py:144
  10.2 132.7 %copy-start.36 = (f32[512]{0:T(512)}, f32[512]{0:T(512)S(1)}, u32[]{:S(2)}) copy-start(f32[512]{0:T(512)S(1)} %broadcast_multiply_fusion.1) | copy-start | bytes 6148
  12.0 122.5 %copy-start.49 = (f32[512]{0:T(512)}, f32[512]{0:T(512)S(1)}, u32[]{:S(2)}) copy-start(f32[512]{0:T(512)S(1)} %fusion.42) | copy-start | bytes 6148
  12.0 130.9 %copy-start.41 = (f32[512]{0:T(512)}, f32[512]{0:T(512)S(1)}, u32[]{:S(2)}) copy-start(f32[512]{0:T(512)S(1)} %fusion.96) | copy-start | bytes 6148
  12.0 130.2 %copy-start.54 = (bf16[6912]{0:T(1024)(128)(2,1)S(1)}, bf16[6912]{0:T(1024)(128)(2,1)}, u32[]{:S(2)}) copy-start(bf16[6912]{0:T(1024)(128)(2,1)} %param.16) | copy-start | bytes 41476
  12.0 130.9 %copy-start.1 = (bf16[512,1,1152]{2,0,1:T(8,128)(2,1)S(1)}, bf16[512,1,1152]{2,0,1:T(8,128)(2,1)}, u32[]{:S(2)}) copy-start(bf16[512,1,1152]{2,0,1:T(8,128)(2,1)} %param.13) | copy-start | bytes 3538948
  142.9 50.3 %copy-start.28 = (f32[1152]{0:T(1024)}, f32[1152]{0:T(1024)S(1)}, u32[]{:S(2)}) copy-start(f32[1152]{0:T(1024)S(1)} %get-tuple-element.50) | copy-start | bytes 13828
  142.9 173.6 %copy-start.33 = (f32[1152]{0:T(1024)}, f32[1152]{0:T(1024)S(1)}, u32[]{:S(2)}) copy-start(f32[1152]{0:T(1024)S(1)} %get-tuple-element.48) | copy-start | bytes 13828
  142.9 383.5 %copy-start.23 = (f32[1152]{0:T(1024)}, f32[1152]{0:T(1024)S(1)}, u32[]{:S(2)}) copy-start(f32[1152]{0:T(1024)S(1)} %get-tuple-element.51) | copy-start | bytes 13828
  144.4 127.9 %all-gather.17.cloned.1.call-start = ((), (), s32[]{:S(2)}) async-start(), calls=%async_computation.11 | async-start | bytes 1566720 | tf_op jit(solution)/shard_map/all_gather | solution.py:126
  145.0 167.5 %reduce-scatter.13.cloned.1.call-start = ((), (), s32[]{:S(2)}) async-start(), calls=%async_computation.12 | async-start | bytes 3538944 | tf_op jit(solution)/shard_map/reduce_scatter | solution.py:166
  231.0 36.1 %copy-start.6 = (bf16[1024,3,576]{0,2,1:T(8,128)(2,1)}, bf16[1024,3,576]{0,2,1:T(8,128)(2,1)S(1)}, u32[]{:S(2)}) copy-start(bf16[1024,3,576]{0,2,1:T(8,128)(2,1)S(1)} %add_convert_fusion) | copy-start | bytes 10616836
  277.6 135.3 %all-gather.19.cloned.1.call-start = ((), (), s32[]{:S(2)}) async-start(), calls=%async_computation.13 | async-start | bytes 3538944 | tf_op jit(solution)/shard_map/all_gather | solution.py:177
  277.7 247.5 %copy-start.25 = (f32[1152]{0:T(1024)}, f32[1152]{0:T(1024)S(1)}, u32[]{:S(2)}) copy-start(f32[1152]{0:T(1024)S(1)} %convert_element_type.196) | copy-start | bytes 13828
  318.3 106.4 %all-gather.21.cloned.1.call-start = ((), (), s32[]{:S(2)}) async-start(), calls=%async_computation.14 | async-start | bytes 5640192 | tf_op jit(solution)/shard_map/all_gather | solution.py:128
  319.1 140.2 %all-gather.23.cloned.1.call-start = ((), (), s32[]{:S(2)}) async-start(), calls=%async_computation.16 | async-start | bytes 3538944 | tf_op jit(solution)/shard_map/all_gather | solution.py:199
  319.1 8.9 collective-permute-start.1
  322.9 9.7 collective-permute-start
  328.1 59.3 %copy-start.15 = (bf16[512,1,1152]{2,0,1:T(8,128)(2,1)S(1)}, bf16[512,1,1152]{2,0,1:T(8,128)(2,1)}, u32[]{:S(2)}) copy-start(bf16[512,1,1152]{2,0,1:T(8,128)(2,1)} %param.25) | copy-start | bytes 3538948
  328.1 59.3 %copy-start.35 = (f32[1152]{0:T(1024)S(1)}, f32[1152]{0:T(1024)}, u32[]{:S(2)}) copy-start(f32[1152]{0:T(1024)} %get-tuple-element.46) | copy-start | bytes 13828
  328.1 9.4 collective-permute-start.3
  332.5 9.6 collective-permute-start.2
  337.5 9.2 collective-permute-start.5
  342.1 9.3 collective-permute-start.4
  346.7 9.3 collective-permute-start.7
  351.4 9.3 collective-permute-start.6
  356.1 9.3 collective-permute-start.9
  360.8 9.4 collective-permute-start.8
  365.4 14.3 %collective-permute-start.11 = (bf16[72,2304]{1,0:T(8,128)(2,1)S(1)}, bf16[72,2304]{1,0:T(8,128)(2,1)}, u32[]{:S(2)}, u32[]{:S(2)}) collective-permute-start(bf16[72,2304]{1,0:T(8,128)(2,1)S(1)} %collective-permute-done.9), channel_id=1, source_target_pairs={{0,30},{2,0},{4,2},{6,4},{8,6},{10,8},{12,10},{14,12},{16,14},{18,... | collective-permute-start | bytes 995336 | tf_op jit(solution)/shard_map/ppermute | solution.py:20
  370.2 15.4 %collective-permute-start.10 = (bf16[72,2304]{1,0:T(8,128)(2,1)S(1)}, bf16[72,2304]{1,0:T(8,128)(2,1)}, u32[]{:S(2)}, u32[]{:S(2)}) collective-permute-start(bf16[72,2304]{1,0:T(8,128)(2,1)S(1)} %collective-permute-done.8), channel_id=1, source_target_pairs={{0,2},{2,4},{4,6},{6,8},{8,10},{10,12},{12,14},{14,16},{16,18},{18... | collective-permute-start | bytes 995336 | tf_op jit(solution)/shard_map/ppermute | solution.py:17
  379.8 21.7 %collective-permute-start.13 = (bf16[72,2304]{1,0:T(8,128)(2,1)}, bf16[72,2304]{1,0:T(8,128)(2,1)}, u32[]{:S(2)}, u32[]{:S(2)}) collective-permute-start(bf16[72,2304]{1,0:T(8,128)(2,1)} %collective-permute-done.11), channel_id=1, source_target_pairs={{0,30},{2,0},{4,2},{6,4},{8,6},{10,8},{12,10},{14,12},{16,14},{18,... | collective-permute-start | bytes 995336 | tf_op jit(solution)/shard_map/ppermute | solution.py:20
  385.6 14.1 %collective-permute-start.12 = (bf16[72,2304]{1,0:T(8,128)(2,1)}, bf16[72,2304]{1,0:T(8,128)(2,1)}, u32[]{:S(2)}, u32[]{:S(2)}) collective-permute-start(bf16[72,2304]{1,0:T(8,128)(2,1)} %collective-permute-done.10), channel_id=1, source_target_pairs={{0,2},{2,4},{4,6},{6,8},{8,10},{10,12},{12,14},{14,16},{16,18},{18... | collective-permute-start | bytes 995336 | tf_op jit(solution)/shard_map/ppermute | solution.py:17
  388.6 133.3 %reduce-scatter.17.cloned.1.call-start = ((), (), s32[]{:S(2)}) async-start(), calls=%async_computation.17 | async-start | bytes 3538944 | tf_op jit(solution)/shard_map/reduce_scatter | solution.py:211
  399.7 12.5 %collective-permute-start.14 = (bf16[72,2304]{1,0:T(8,128)(2,1)}, bf16[72,2304]{1,0:T(8,128)(2,1)S(1)}, u32[]{:S(2)}, u32[]{:S(2)}) collective-permute-start(bf16[72,2304]{1,0:T(8,128)(2,1)} %collective-permute-done.12), channel_id=1, source_target_pairs={{0,2},{2,4},{4,6},{6,8},{8,10},{10,12},{12,14},{14,16},{16,18},{18... | collective-permute-start | bytes 995336 | tf_op jit(solution)/shard_map/ppermute | solution.py:17
  487.0 79.2 %all-gather.25.cloned.1.call-start = ((), (), s32[]{:S(2)}) async-start(), calls=%async_computation.18 | async-start | bytes 3538944 | tf_op jit(solution)/shard_map/all_gather | solution.py:228
  529.9 233.5 %reduce-scatter.23.cloned.1.call-start = ((), (), s32[]{:S(2)}) async-start(), calls=%async_computation.21 | async-start | bytes 5640192 | tf_op jit(solution)/shard_map/reduce_scatter | solution.py:291
  540.9 224.4 %reduce-scatter.21.cloned.1.call-start = ((), (), s32[]{:S(2)}) async-start(), calls=%async_computation.20 | async-start | bytes 5640192 | tf_op jit(solution)/shard_map/reduce_scatter | solution.py:288
  552.3 242.3 %reduce-scatter.27.cloned.1.call-start = ((), (), s32[]{:S(2)}) async-start(), calls=%async_computation.23 | async-start | bytes 1566720
  662.8 167.6 %reduce-scatter.19.cloned.1.call-start = ((), (), s32[]{:S(2)}) async-start(), calls=%async_computation.19 | async-start | bytes 3538944 | tf_op jit(solution)/shard_map/reduce_scatter | solution.py:246
  680.3 187.1 %reduce-scatter.15.cloned.1.call-start = ((), (), s32[]{:S(2)}) async-start(), calls=%async_computation.15 | async-start | bytes 3538944 | tf_op jit(solution)/shard_map/reduce_scatter | solution.py:186
  694.9 278.8 %reduce-scatter.25.cloned.1.call-start = ((), (), s32[]{:S(2)}) async-start(), calls=%async_computation.22 | async-start | bytes 4386816
  759.7 74.2 %copy-start.2 = (bf16[512,1,1152]{2,0,1:T(8,128)(2,1)S(1)}, bf16[512,1,1152]{2,0,1:T(8,128)(2,1)}, u32[]{:S(2)}) copy-start(bf16[512,1,1152]{2,0,1:T(8,128)(2,1)} %param.13) | copy-start | bytes 3538948
  765.3 102.1 %copy-start.5 = (bf16[512,1152]{1,0:T(8,128)(2,1)S(1)}, bf16[512,1152]{1,0:T(8,128)(2,1)}, u32[]{:S(2)}) copy-start(bf16[512,1152]{1,0:T(8,128)(2,1)} %reduce-scatter.13.cloned.1.call-done) | copy-start | bytes 3538948
  765.3 102.1 %copy-start.24 = (f32[1152]{0:T(1024)S(1)}, f32[1152]{0:T(1024)}, u32[]{:S(2)}) copy-start(f32[1152]{0:T(1024)} %copy-done.23) | copy-start | bytes 13828
  765.3 102.1 %copy-start.26 = (f32[1152]{0:T(1024)S(1)}, f32[1152]{0:T(1024)}, u32[]{:S(2)}) copy-start(f32[1152]{0:T(1024)} %copy-done.25) | copy-start | bytes 13828
  (59 other events, 563.6 us)
Sparse Core Ops, SparseCore 0:
  10.2 124.2 all-gather.10
  136.6 49.9 all-gather.14
  188.7 34.5 all-gather.12
  225.3 39.3 all-gather.16
  277.8 34.7 reduce-scatter.12
  318.5 36.0 all-gather.18
  357.0 60.6 all-gather.20
  419.9 39.4 all-gather.22
  487.1 34.6 reduce-scatter.16
  530.1 36.0 all-gather.24
  570.2 79.8 reduce-scatter.22
  654.0 78.4 reduce-scatter.20
  736.7 57.8 reduce-scatter.26
  796.8 33.6 reduce-scatter.18
  832.6 34.6 reduce-scatter.14
  871.1 73.1 reduce-scatter.24
